TPU v7x, 32 devices: a whole 2x2x4 slice. The times are simulated.
32 devices in a mesh: region: 16 (over z, x, core), sub: 2 (over y).
Axes of the slice: x: 2, y: 2, z: 4, core: 2. Of those that a mesh axis runs over, the one named last changes fastest.
Arguments:
- source: float32 [8, 8, 8, 8192], P(None, None, None, ('region', 'sub')), may hold values from -3.5 to 4.5
- metric: float32 [3, 8, 8, 8, 8192], P(None, None, None, None, ('region', 'sub')), may hold values from 0.002 to 0.008
- face_area: float32 [6, 8192], P(None, ('region', 'sub')), may hold values from 0.5 to 13.5
- outlet_gain: float32 [8], replicated, may hold values from 0.0018310547 to 0.0073242188
- neighbour: int32 [6, 8192], P(None, ('region', 'sub')), may hold values from 0 to 2048, as said below
- orient: int32 [6, 8192], P(None, ('region', 'sub')), may hold values from 0 to 7
- outlet: int32 [6, 8192], P(None, ('region', 'sub')), may hold values from 0 to 8, as said below
- export_list: int32 [128, 128], P(('region', 'sub')), may hold values from 0 to 1535, as said below
Outputs:
- solution: float32 [8, 8, 8, 8192], P(None, None, None, ('region', 'sub'))
- residual: float32 [8, 8, 8, 8192], P(None, None, None, ('region', 'sub'))
Inputs may be any that keep to these rules, and one draw needn't show every extreme that they name: Values below 1536 name the device's own faces, the next 128 each the four received lists in pool order; 2048 means the face has no neighbour, as on every outlet face and for any list from a device outside the mesh. 8 means the face belongs to no outlet. `export_list`: each row holds 128 different local face numbers.
All inputs are finite; a program needn't handle non-finite values.
Results may differ from a plain program's by a relative error of at most 0.0001.
Values sent between devices are 32-bit elements; how exact they have to be, the bound alone decides.
A program may use at most 64 MiB of HBM per device.

v0:
```python
import functools

import jax
import jax.numpy as jnp
import numpy as np
from jax import lax
from jax.experimental import pallas as pl
from jax.experimental.pallas import tpu as pltpu
from jax.sharding import PartitionSpec as P

NP = 8
ITERS = 4
MESH = pl.DeviceIdType.MESH
F32 = jnp.float32
BF16 = jnp.bfloat16

GLL_POINTS = np.array(
    [
        -1.0,
        -0.8717401485096066,
        -0.5917001814331423,
        -0.2092992179024789,
        0.2092992179024789,
        0.5917001814331423,
        0.8717401485096066,
        1.0,
    ]
)


def legendre_seven(points):
    previous = points * 0.0 + 1.0
    current = points * 1.0
    for degree in range(1, 7):
        previous, current = (
            current,
            ((2 * degree + 1) * points * current - degree * previous) / (degree + 1),
        )
    return current


def node_tables():
    values = legendre_seven(GLL_POINTS)
    weights = 2.0 / (56.0 * values * values)
    equal = (GLL_POINTS[:, None] == GLL_POINTS[None, :]) * 1.0
    differ = GLL_POINTS[:, None] - GLL_POINTS[None, :] + equal
    deriv = values[:, None] / (values[None, :] * differ) * (1.0 - equal)
    deriv[0, 0] = -14.0
    deriv[7, 7] = 14.0
    return deriv, weights


DERIV, WEIGHTS = node_tables()
DERIV = DERIV.astype(np.float32).astype(np.float64)


def split_table(table):
    table = np.kron(np.eye(NP), table)
    high = table.astype(jnp.bfloat16).astype(np.float64)
    return np.concatenate([high, high, table - high], axis=1)


def turn_variants():
    grid = np.arange(NP * NP).reshape(NP, NP)
    forms = [grid, grid[:, ::-1], grid.T, grid.T[:, ::-1]]
    table = np.zeros((4 * NP * NP, NP * NP))
    for form, moved in enumerate(forms):
        for place, origin in enumerate(moved.reshape(-1)):
            table[form * NP * NP + place, origin] = 1.0
    return np.concatenate([table, table], axis=1)


def small_apply(table, parts, sign):
    half = NP // 2
    even = [parts[i] + parts[NP - 1 - i] for i in range(half)]
    odd = [parts[i] - parts[NP - 1 - i] for i in range(half)]
    out = [None] * NP
    for a in range(half):
        p = q = None
        for i in range(half):
            plus = float(0.5 * (table[a, i] + table[a, NP - 1 - i])) * even[i]
            minus = float(0.5 * (table[a, i] - table[a, NP - 1 - i])) * odd[i]
            p = plus if p is None else p + plus
            q = minus if q is None else q + minus
        out[a] = p + q
        out[NP - 1 - a] = p - q if sign > 0 else q - p
    return out


def split(x):
    high = x.astype(BF16)
    low = (x - high.astype(F32)).astype(BF16)
    return high, low


def along_k(table, x):
    high, low = split(x)
    return jnp.dot(table, jnp.concatenate([high, low, high], axis=0), preferred_element_type=F32)


def kernel(
    n_region,
    n_sub,
    source,
    metric,
    face_area,
    gain,
    neighbour,
    orient,
    outlet,
    export_list,
    tables,
    turner,
    sol,
    res,
    field,
    direction,
    inverse,
    pool,
    export_hot,
    link_hot,
    got,
    send_buf,
    recv_buf,
    sub_part,
    sub_recv,
    reg_part,
    reg_recv,
    ex_send,
    ex_recv,
    sub_send_sem,
    sub_recv_sem,
    reg_send_sem,
    reg_recv_sem,
):
    elems = source.shape[3]
    slots = export_list.shape[1]
    own = 6 * elems
    region = lax.axis_index("region")
    sub = lax.axis_index("sub")
    square = DERIV * DERIV

    recv_buf[...] = jnp.zeros_like(recv_buf)

    barrier = pltpu.get_barrier_semaphore()

    @pl.loop(1, n_region)
    def _(k):
        peer = lax.rem(region + k, n_region)
        pl.semaphore_signal(barrier, inc=1, device_id={"region": peer, "sub": sub}, device_id_type=MESH)

    @pl.loop(1, n_sub)
    def _(k):
        peer = lax.rem(sub + k, n_sub)
        pl.semaphore_signal(barrier, inc=1, device_id={"region": region, "sub": peer}, device_id_type=MESH)

    chunk = 64

    @pl.loop(0, own // chunk)
    def _(p):
        start = pl.multiple_of(p * chunk, chunk)
        rows = lax.broadcasted_iota(jnp.int32, (chunk, slots), 0) + start
        for r in range(4):
            hit = jnp.where(rows == export_list[r : r + 1, :], 1.0, 0.0)
            export_hot[pl.ds(start, chunk), r * slots : (r + 1) * slots] = hit.astype(BF16)

    def build_links():
        @pl.loop(0, link_hot.shape[1] // chunk)
        def _(p):
            start = pl.multiple_of(p * chunk, chunk)
            rows = lax.broadcasted_iota(jnp.int32, (chunk, elems), 0) + start
            for f in range(6):
                hit = jnp.where(rows == neighbour[f : f + 1, :], 1.0, 0.0)
                link_hot[f, pl.ds(start, chunk), :] = hit.astype(BF16)

    routes = (
        (1, sub < n_sub - 1, {"region": region, "sub": jnp.minimum(sub + 1, n_sub - 1)}, sub > 0),
        (0, sub > 0, {"region": region, "sub": jnp.maximum(sub - 1, 0)}, sub < n_sub - 1),
        (3, region < n_region - 1, {"region": jnp.minimum(region + 1, n_region - 1), "sub": sub}, region > 0),
        (2, region > 0, {"region": jnp.maximum(region - 1, 0), "sub": sub}, region < n_region - 1),
    )

    def copy_of(turn, slot):
        row, _, peer, _ = routes[slot]
        return pltpu.make_async_remote_copy(
            src_ref=send_buf.at[turn, row],
            dst_ref=recv_buf.at[turn, slot],
            send_sem=ex_send.at[turn, slot],
            recv_sem=ex_recv.at[turn, slot],
            device_id=peer,
            device_id_type=MESH,
        )

    k_id = lax.broadcasted_iota(jnp.int32, (NP, elems), 0)
    lowest = k_id == 0
    highest = k_id == NP - 1

    def exchange(turn):
        def put(f, block):
            high, low = split(block)
            pool[0:64, f * elems : (f + 1) * elems] = high
            pool[64:128, f * elems : (f + 1) * elems] = low

        put(0, field[0].reshape(64, elems))
        put(1, field[NP - 1].reshape(64, elems))
        put(2, jnp.concatenate([field[i, 0] for i in range(NP)], axis=0))
        put(3, jnp.concatenate([field[i, NP - 1] for i in range(NP)], axis=0))
        for f, k in ((4, 0), (5, NP - 1)):
            rows = []
            for i in range(NP):
                block = jnp.broadcast_to(field[i, 0, k : k + 1, :], (NP, elems))
                for j in range(1, NP):
                    block = jnp.where(k_id == j, field[i, j, k : k + 1, :], block)
                rows.append(block)
            put(f, jnp.concatenate(rows, axis=0))
        both = jnp.dot(pool[...], export_hot[...], preferred_element_type=F32)
        sent = both[0:64] + both[64:128]
        for r in range(4):
            send_buf[turn, r] = sent[:, r * slots : (r + 1) * slots]
        for slot in range(4):

            @pl.when(routes[slot][1])
            def _(slot=slot):
                copy_of(turn, slot).start()

    def own_part():
        @pl.loop(0, 6)
        def _(f):
            got[f] = jnp.dot(pool[...], link_hot[f, 0:own, :], preferred_element_type=F32)

    def finish(turn, coeff):
        for slot in range(4):

            @pl.when(routes[slot][3])
            def _(slot=slot):
                copy_of(turn, slot).wait_recv()

            @pl.when(routes[slot][1])
            def _(slot=slot):
                copy_of(turn, slot).wait_send()

        arrived = jnp.concatenate([recv_buf[turn, s] for s in range(4)], axis=1)
        high, low = split(arrived)
        arrived = jnp.concatenate([high, low], axis=0)
        w_col = jnp.zeros((NP, elems), F32)
        for b in range(NP):
            w_col = jnp.where(k_id == b, float(WEIGHTS[b]), w_col)
        held = []
        for f in range(6):
            fetched = got[f] + jnp.dot(
                arrived, link_hot[f, own:, :], preferred_element_type=F32
            )
            forms = jnp.dot(turner[...], fetched.astype(BF16), preferred_element_type=F32)
            code = jnp.broadcast_to(orient[f : f + 1, :], (NP, elems))
            bit0 = (code & 1) == 1
            bit1 = (code & 2) == 2
            bit2 = (code & 4) == 4
            is_turned = bit2
            reversed_cols = ((code & 6) == 2) | ((code & 5) == 5)
            flip = ((code & 5) == 1) | ((code & 6) == 6)
            base = []
            for a in range(NP):
                form = [forms[m * 64 + a * NP : m * 64 + a * NP + NP] for m in range(4)]
                base.append(
                    jnp.where(
                        is_turned,
                        jnp.where(reversed_cols, form[3], form[2]),
                        jnp.where(reversed_cols, form[1], form[0]),
                    )
                )
            out = [jnp.where(flip, base[NP - 1 - a], base[a]) for a in range(NP)]
            if coeff is not None:
                spread = coeff[f] * w_col
                out = [out[a] + float(WEIGHTS[a]) * spread for a in range(NP)]
            if f < 2:
                for a in range(NP):
                    field[f * (NP - 1), a] += out[a]
            elif f < 4:
                for a in range(NP):
                    field[a, (f - 2) * (NP - 1)] += out[a]
            else:
                held.append(out)
        for a in range(NP):
            for j in range(NP):
                extra = jnp.where(
                    lowest,
                    held[0][a][j : j + 1, :],
                    jnp.where(highest, held[1][a][j : j + 1, :], 0.0),
                )
                field[a, j] += extra

    for t in range(NP):
        out = small_apply(square.T, [metric[0, a, t] for a in range(NP)], 1)
        for i in range(NP):
            field[i, t] = out[i]
    for t in range(NP):
        out = small_apply(square.T, [metric[1, t, b] for b in range(NP)], 1)
        along = along_k(tables[2], metric[2, t].reshape(64, elems)).reshape(NP, NP, elems)
        for j in range(NP):
            field[t, j] += out[j] + along[j]

    pl.semaphore_wait(barrier, n_region + n_sub - 2)

    exchange(0)
    build_links()
    own_part()
    finish(0, None)

    ratio = 4.5 / 3.5

    @pl.loop(0, NP)
    def _(t):
        inv = 1.0 / field[t]
        inverse[t] = inv
        first = inv * source[t] / 4.5
        direction[t] = first
        sol[t] = first
        res[t] = source[t]

    lanes = 128
    o_id = lax.broadcasted_iota(jnp.int32, (NP, elems), 0)
    diag = lax.broadcasted_iota(jnp.int32, (NP, lanes), 0) == lax.broadcasted_iota(
        jnp.int32, (NP, lanes), 1
    )

    def sub_copy(it, peer, owner):
        return pltpu.make_async_remote_copy(
            src_ref=sub_part.at[it],
            dst_ref=sub_recv.at[it, owner],
            send_sem=sub_send_sem.at[it, peer],
            recv_sem=sub_recv_sem.at[it, owner],
            device_id={"region": region, "sub": peer},
            device_id_type=MESH,
        )

    def reg_copy(it, peer, owner):
        return pltpu.make_async_remote_copy(
            src_ref=reg_part.at[it],
            dst_ref=reg_recv.at[it, owner],
            send_sem=reg_send_sem.at[it, peer],
            recv_sem=reg_recv_sem.at[it, owner],
            device_id={"region": peer, "sub": sub},
            device_id_type=MESH,
        )

    def flux_start(it):
        w_col = jnp.zeros((NP, elems), F32)
        for b in range(NP):
            w_col = jnp.where(k_id == b, float(WEIGHTS[b]), w_col)

        def line(parts):
            total = float(WEIGHTS[0]) * parts[0]
            for a in range(1, NP):
                total = total + float(WEIGHTS[a]) * parts[a]
            return total

        sums = []
        for i in (0, NP - 1):
            sums.append(line([direction[i, a] for a in range(NP)]))
        for j in (0, NP - 1):
            sums.append(line([direction[a, j] for a in range(NP)]))
        sums = [jnp.sum(s * w_col, axis=0, keepdims=True) for s in sums]
        whole = line([line([direction[i, j] for j in range(NP)]) for i in range(NP)])
        sums += [whole[0:1], whole[NP - 1 : NP]]
        total = jnp.zeros((NP, elems), F32)
        for f in range(6):
            part = face_area[f : f + 1, :] * sums[f]
            total = total + jnp.where(outlet[f : f + 1, :] == o_id, part, 0.0)
        column = jnp.sum(total, axis=1, keepdims=True)
        row = jnp.sum(jnp.where(diag, column, 0.0), axis=0, keepdims=True)
        sub_part[it] = row

        @pl.loop(1, n_sub)
        def _(k):
            peer = lax.rem(sub + k, n_sub)
            sub_copy(it, peer, sub).start()

    def flux_middle(it):
        def more(k, total):
            owner = lax.rem(sub + k, n_sub)
            sub_copy(it, owner, owner).wait()
            return total + sub_recv[it, owner]

        total = lax.fori_loop(1, n_sub, more, sub_part[it])
        reg_part[it] = total

        @pl.loop(1, n_region)
        def _(k):
            peer = lax.rem(region + k, n_region)
            reg_copy(it, peer, region).start()

    def flux_end(it):
        def more(k, total):
            owner = lax.rem(region + k, n_region)
            reg_copy(it, owner, owner).wait()
            return total + reg_recv[it, owner]

        row = lax.fori_loop(1, n_region, more, reg_part[it])
        scaled = row * gain[...]
        column = jnp.sum(
            jnp.where(diag, jnp.broadcast_to(scaled, (NP, lanes)), 0.0), axis=1, keepdims=True
        )
        coeff = []
        for f in range(6):
            picked = jnp.sum(
                jnp.where(outlet[f : f + 1, :] == o_id, column, 0.0), axis=0, keepdims=True
            )
            coeff.append(picked * face_area[f : f + 1, :])
        return coeff

    def stiffness():
        for t in range(NP):
            grads = small_apply(DERIV, [direction[i, t] for i in range(NP)], -1)
            grads = [grads[a] * metric[0, a, t] for a in range(NP)]
            out = small_apply(DERIV.T, grads, -1)
            for i in range(NP):
                field[i, t] = out[i]
        for t in range(NP):
            along = along_k(tables[0], direction[t].reshape(64, elems))
            along = along * metric[2, t].reshape(64, elems)
            along = along_k(tables[1], along).reshape(NP, NP, elems)
            grads = small_apply(DERIV, [direction[t, j] for j in range(NP)], -1)
            grads = [grads[b] * metric[1, t, b] for b in range(NP)]
            out = small_apply(DERIV.T, grads, -1)
            for j in range(NP):
                field[t, j] += out[j] + along[j]

    rho = 1.0 / ratio
    scales = []
    for it in range(ITERS):
        rho_next = 1.0 / (2.0 * ratio - rho)
        scales.append((rho_next * rho, 2.0 * rho_next / 3.5))
        rho = rho_next

    @pl.loop(0, ITERS)
    def _(it):
        keep, gain_now = (jnp.float32(scales[0][0]), jnp.float32(scales[0][1]))
        for step in range(1, ITERS):
            keep = jnp.where(it == step, jnp.float32(scales[step][0]), keep)
            gain_now = jnp.where(it == step, jnp.float32(scales[step][1]), gain_now)
        flux_start(it)
        stiffness()
        flux_middle(it)
        exchange(it + 1)
        own_part()
        finish(it + 1, flux_end(it))

        @pl.loop(0, NP)
        def _(t):
            left = res[t] - field[t]
            res[t] = left
            fresh = keep * direction[t] + gain_now * inverse[t] * left
            direction[t] = fresh
            sol[t] = sol[t] + fresh


def per_device(n_region, n_sub, source, metric, face_area, outlet_gain, neighbour, orient, outlet, export_list):
    elems = source.shape[3]
    slots = export_list.shape[1]
    own = 6 * elems
    full = own + 4 * slots
    outlets = outlet_gain.shape[0]
    gain = jnp.pad(outlet_gain.reshape(1, outlets), ((0, 0), (0, 128 - outlets)))
    square = DERIV * DERIV
    tables = jnp.asarray(
        np.stack([split_table(DERIV), split_table(DERIV.T), split_table(square.T)]), BF16
    )
    turner = jnp.asarray(turn_variants(), BF16)
    shape = jax.ShapeDtypeStruct(source.shape, F32)
    vmem = pl.BlockSpec(memory_space=pltpu.VMEM)
    dma = pltpu.SemaphoreType.DMA
    return pl.pallas_call(
        functools.partial(kernel, n_region, n_sub),
        out_shape=(shape, shape),
        in_specs=[vmem] * 10,
        out_specs=(vmem, vmem),
        scratch_shapes=[
            pltpu.VMEM(source.shape, F32),
            pltpu.VMEM(source.shape, F32),
            pltpu.VMEM(source.shape, F32),
            pltpu.VMEM((128, own), BF16),
            pltpu.VMEM((own, 4 * slots), BF16),
            pltpu.VMEM((6, full, elems), BF16),
            pltpu.VMEM((6, 128, elems), F32),
            pltpu.VMEM((ITERS + 1, 4, 64, slots), F32),
            pltpu.VMEM((ITERS + 1, 4, 64, slots), F32),
            pltpu.VMEM((ITERS, 1, 128), F32),
            pltpu.VMEM((ITERS, n_sub, 1, 128), F32),
            pltpu.VMEM((ITERS, 1, 128), F32),
            pltpu.VMEM((ITERS, n_region, 1, 128), F32),
            dma((ITERS + 1, 4)),
            dma((ITERS + 1, 4)),
            dma((ITERS, n_sub)),
            dma((ITERS, n_sub)),
            dma((ITERS, n_region)),
            dma((ITERS, n_region)),
        ],
        compiler_params=pltpu.CompilerParams(collective_id=0, has_side_effects=True),
    )(source, metric, face_area, gain, neighbour, orient, outlet, export_list, tables, turner)


def solution(mesh):
    placed = (
        P(None, None, None, ("region", "sub")),
        P(None, None, None, None, ("region", "sub")),
        P(None, ("region", "sub")),
        P(),
        P(None, ("region", "sub")),
        P(None, ("region", "sub")),
        P(None, ("region", "sub")),
        P(("region", "sub"), None),
    )
    field = P(None, None, None, ("region", "sub"))
    return jax.shard_map(
        functools.partial(per_device, mesh.shape["region"], mesh.shape["sub"]),
        mesh=mesh,
        in_specs=placed,
        out_specs=(field, field),
        check_vma=False,
    )
```

profile of v0, /device:TPU:0, one launch (start us, length us, event | category | flops | bytes accessed | tf_op | source)
XLA Modules:
  0.0 52.9 jit_solution(1319252648324872035)
XLA Ops:
  0.6 1.2 %pad.4.gain = f32[1,128]{1,0:T(1,128)} pad(f32[1,8]{1,0:T(1,128)} %bitcast.1, f32[]{:T(128)} %constant.6.clone.1), padding=0_0x0_120 | pad | bytes 548 | tf_op jit(solution)/shard_map/jit(_pad)/pad | solution.py:463
  1.8 47.4 %shard_map.113 = (f32[8,8,8,256]{3,2,1,0:T(8,128)}, f32[8,8,8,256]{3,2,1,0:T(8,128)}) custom-call(f32[8,8,8,256]{3,2,1,0:T(8,128)} %source.1, f32[3,8,8,8,256]{4,3,2,1,0:T(8,128)} %metric.1, f32[6,256]{1,0:T(8,128)} %face_area.1, f32[1,128]{1,0:T(1,128)} %pad.4.gain, s32[6,256]{1,0:T(8,128)} %neighbour.1, s32[6,256]{1,0:T(8,128)} %orient.1, ...), custom_call_target="tpu_custom_call" | custom-call | tf_op jit(solution)/shard_map/pallas_call | solution.py:472
  49.2 1.9 %copy.14 = f32[8,8,8,256]{3,2,1,0:T(8,128)} copy(f32[8,8,8,256]{3,2,1,0:T(8,128)} %get-tuple-element.4) | data formatting | bytes 1048576
  51.1 1.9 %copy.15 = f32[8,8,8,256]{3,2,1,0:T(8,128)} copy(f32[8,8,8,256]{3,2,1,0:T(8,128)} %get-tuple-element.5) | data formatting | bytes 1048576
where the time goes:
time: 53.2 us; the launch traced here: 52.9 us
  Pallas kernels  47.4 us (89%)
  local copies, waits for them, and re-layouts  4.91 us (9%)
  between operations  0.64 us (1%)
    pallas_call x1, Pallas kernels, per_device(): pl.pallas_call(functools.partial(kernel, n_region, n_sub), out_shape=(sha...  47.4 us
    unnamed x2, local copies, waits for them, and re-layouts  3.74 us
    pad x1, local copies, waits for them, and re-layouts, per_device(): jnp.pad(outlet_gain.reshape(1, outlets), ((0, 0), (0, 128 - outlets)))  1.17 us

commit v1 on v0

--- a/solution.py
+++ b/solution.py
@@ -101,8 +101,8 @@
 def kernel(
     n_region,
     n_sub,
-    source,
-    metric,
+    source_hbm,
+    metric_hbm,
     face_area,
     gain,
     neighbour,
@@ -113,6 +113,7 @@
     turner,
     sol,
     res,
+    metric,
     field,
     direction,
     inverse,
@@ -122,37 +123,43 @@
     got,
     send_buf,
     recv_buf,
-    sub_part,
-    sub_recv,
-    reg_part,
-    reg_recv,
+    flux_part,
+    flux_recv,
     ex_send,
     ex_recv,
-    sub_send_sem,
-    sub_recv_sem,
-    reg_send_sem,
-    reg_recv_sem,
+    flux_send_sem,
+    flux_recv_sem,
+    load_sem,
 ):
-    elems = source.shape[3]
+    elems = res.shape[3]
     slots = export_list.shape[1]
     own = 6 * elems
     region = lax.axis_index("region")
     sub = lax.axis_index("sub")
     square = DERIV * DERIV
+    devices = n_region * n_sub
+    me = region * n_sub + sub
+
+    loads = [
+        pltpu.make_async_copy(metric_hbm.at[0], metric.at[0], load_sem.at[0]),
+        pltpu.make_async_copy(metric_hbm.at[1], metric.at[1], load_sem.at[1]),
+        pltpu.make_async_copy(metric_hbm.at[2], metric.at[2], load_sem.at[2]),
+        pltpu.make_async_copy(source_hbm, res, load_sem.at[3]),
+    ]
+    for load in loads:
+        load.start()
 
     recv_buf[...] = jnp.zeros_like(recv_buf)
 
     barrier = pltpu.get_barrier_semaphore()
 
-    @pl.loop(1, n_region)
+    def peer_at(k):
+        peer = lax.rem(me + k, devices)
+        return {"region": lax.div(peer, n_sub), "sub": lax.rem(peer, n_sub)}
+
+    @pl.loop(1, devices)
     def _(k):
-        peer = lax.rem(region + k, n_region)
-        pl.semaphore_signal(barrier, inc=1, device_id={"region": peer, "sub": sub}, device_id_type=MESH)
-
-    @pl.loop(1, n_sub)
-    def _(k):
-        peer = lax.rem(sub + k, n_sub)
-        pl.semaphore_signal(barrier, inc=1, device_id={"region": region, "sub": peer}, device_id_type=MESH)
+        pl.semaphore_signal(barrier, inc=1, device_id=peer_at(k), device_id_type=MESH)
 
     chunk = 64
 
@@ -228,7 +235,7 @@
         def _(f):
             got[f] = jnp.dot(pool[...], link_hot[f, 0:own, :], preferred_element_type=F32)
 
-    def finish(turn, coeff):
+    def finish(turn):
         for slot in range(4):
 
             @pl.when(routes[slot][3])
@@ -242,9 +249,6 @@
         arrived = jnp.concatenate([recv_buf[turn, s] for s in range(4)], axis=1)
         high, low = split(arrived)
         arrived = jnp.concatenate([high, low], axis=0)
-        w_col = jnp.zeros((NP, elems), F32)
-        for b in range(NP):
-            w_col = jnp.where(k_id == b, float(WEIGHTS[b]), w_col)
         held = []
         for f in range(6):
             fetched = got[f] + jnp.dot(
@@ -269,9 +273,6 @@
                     )
                 )
             out = [jnp.where(flip, base[NP - 1 - a], base[a]) for a in range(NP)]
-            if coeff is not None:
-                spread = coeff[f] * w_col
-                out = [out[a] + float(WEIGHTS[a]) * spread for a in range(NP)]
             if f < 2:
                 for a in range(NP):
                     field[f * (NP - 1), a] += out[a]
@@ -289,33 +290,36 @@
                 )
                 field[a, j] += extra
 
+    loads[0].wait()
     for t in range(NP):
         out = small_apply(square.T, [metric[0, a, t] for a in range(NP)], 1)
         for i in range(NP):
             field[i, t] = out[i]
+    loads[1].wait()
+    loads[2].wait()
     for t in range(NP):
         out = small_apply(square.T, [metric[1, t, b] for b in range(NP)], 1)
         along = along_k(tables[2], metric[2, t].reshape(64, elems)).reshape(NP, NP, elems)
         for j in range(NP):
             field[t, j] += out[j] + along[j]
 
-    pl.semaphore_wait(barrier, n_region + n_sub - 2)
+    pl.semaphore_wait(barrier, devices - 1)
 
     exchange(0)
     build_links()
     own_part()
-    finish(0, None)
+    finish(0)
 
     ratio = 4.5 / 3.5
+    loads[3].wait()
 
     @pl.loop(0, NP)
     def _(t):
         inv = 1.0 / field[t]
         inverse[t] = inv
-        first = inv * source[t] / 4.5
+        first = inv * res[t] / 4.5
         direction[t] = first
         sol[t] = first
-        res[t] = source[t]
 
     lanes = 128
     o_id = lax.broadcasted_iota(jnp.int32, (NP, elems), 0)
@@ -323,30 +327,11 @@
         jnp.int32, (NP, lanes), 1
     )
 
-    def sub_copy(it, peer, owner):
-        return pltpu.make_async_remote_copy(
-            src_ref=sub_part.at[it],
-            dst_ref=sub_recv.at[it, owner],
-            send_sem=sub_send_sem.at[it, peer],
-            recv_sem=sub_recv_sem.at[it, owner],
-            device_id={"region": region, "sub": peer},
-            device_id_type=MESH,
-        )
-
-    def reg_copy(it, peer, owner):
-        return pltpu.make_async_remote_copy(
-            src_ref=reg_part.at[it],
-            dst_ref=reg_recv.at[it, owner],
-            send_sem=reg_send_sem.at[it, peer],
-            recv_sem=reg_recv_sem.at[it, owner],
-            device_id={"region": peer, "sub": sub},
-            device_id_type=MESH,
-        )
+    w_col = jnp.zeros((NP, elems), F32)
+    for b in range(NP):
+        w_col = jnp.where(k_id == b, float(WEIGHTS[b]), w_col)
 
     def flux_start(it):
-        w_col = jnp.zeros((NP, elems), F32)
-        for b in range(NP):
-            w_col = jnp.where(k_id == b, float(WEIGHTS[b]), w_col)
 
         def line(parts):
             total = float(WEIGHTS[0]) * parts[0]
@@ -368,38 +353,32 @@
             total = total + jnp.where(outlet[f : f + 1, :] == o_id, part, 0.0)
         column = jnp.sum(total, axis=1, keepdims=True)
         row = jnp.sum(jnp.where(diag, column, 0.0), axis=0, keepdims=True)
-        sub_part[it] = row
-
-        @pl.loop(1, n_sub)
+        flux_part[it] = row
+
+        @pl.loop(1, devices)
         def _(k):
-            peer = lax.rem(sub + k, n_sub)
-            sub_copy(it, peer, sub).start()
-
-    def flux_middle(it):
-        def more(k, total):
-            owner = lax.rem(sub + k, n_sub)
-            sub_copy(it, owner, owner).wait()
-            return total + sub_recv[it, owner]
-
-        total = lax.fori_loop(1, n_sub, more, sub_part[it])
-        reg_part[it] = total
-
-        @pl.loop(1, n_region)
-        def _(k):
-            peer = lax.rem(region + k, n_region)
-            reg_copy(it, peer, region).start()
+            pltpu.make_async_remote_copy(
+                src_ref=flux_part.at[it],
+                dst_ref=flux_recv.at[it, k - 1],
+                send_sem=flux_send_sem.at[it],
+                recv_sem=flux_recv_sem.at[it],
+                device_id=peer_at(k),
+                device_id_type=MESH,
+            ).start()
 
     def flux_end(it):
-        def more(k, total):
-            owner = lax.rem(region + k, n_region)
-            reg_copy(it, owner, owner).wait()
-            return total + reg_recv[it, owner]
-
-        row = lax.fori_loop(1, n_region, more, reg_part[it])
-        scaled = row * gain[...]
+        every = flux_recv.at[it]
+        pltpu.make_async_copy(every, every, flux_recv_sem.at[it]).wait()
+        pltpu.make_async_copy(every, every, flux_send_sem.at[it]).wait()
+        row = flux_part[it] + jnp.sum(flux_recv[it], axis=0)
         column = jnp.sum(
-            jnp.where(diag, jnp.broadcast_to(scaled, (NP, lanes)), 0.0), axis=1, keepdims=True
+            jnp.where(diag, jnp.broadcast_to(row, (NP, lanes)), 0.0), axis=1, keepdims=True
         )
+        gains = jnp.zeros((NP, lanes), F32)
+        g_id = lax.broadcasted_iota(jnp.int32, (NP, lanes), 0)
+        for o in range(gain.shape[0]):
+            gains = jnp.where(g_id == o, gain[o], gains)
+        column = column * gains[:, 0:1]
         coeff = []
         for f in range(6):
             picked = jnp.sum(
@@ -440,18 +419,28 @@
             gain_now = jnp.where(it == step, jnp.float32(scales[step][1]), gain_now)
         flux_start(it)
         stiffness()
-        flux_middle(it)
         exchange(it + 1)
         own_part()
-        finish(it + 1, flux_end(it))
-
-        @pl.loop(0, NP)
-        def _(t):
-            left = res[t] - field[t]
-            res[t] = left
-            fresh = keep * direction[t] + gain_now * inverse[t] * left
-            direction[t] = fresh
-            sol[t] = sol[t] + fresh
+        finish(it + 1)
+        coeff = flux_end(it)
+        ends = jnp.where(lowest, coeff[4], jnp.where(highest, coeff[5], 0.0))
+        sides = [coeff[f] * w_col for f in range(4)]
+        for i in range(NP):
+            for j in range(NP):
+                extra = float(WEIGHTS[i] * WEIGHTS[j]) * ends
+                if i == 0:
+                    extra = extra + float(WEIGHTS[j]) * sides[0]
+                if i == NP - 1:
+                    extra = extra + float(WEIGHTS[j]) * sides[1]
+                if j == 0:
+                    extra = extra + float(WEIGHTS[i]) * sides[2]
+                if j == NP - 1:
+                    extra = extra + float(WEIGHTS[i]) * sides[3]
+                left = res[i, j] - field[i, j] - extra
+                res[i, j] = left
+                fresh = keep * direction[i, j] + gain_now * inverse[i, j] * left
+                direction[i, j] = fresh
+                sol[i, j] = sol[i, j] + fresh
 
 
 def per_device(n_region, n_sub, source, metric, face_area, outlet_gain, neighbour, orient, outlet, export_list):
@@ -459,22 +448,23 @@
     slots = export_list.shape[1]
     own = 6 * elems
     full = own + 4 * slots
-    outlets = outlet_gain.shape[0]
-    gain = jnp.pad(outlet_gain.reshape(1, outlets), ((0, 0), (0, 128 - outlets)))
     square = DERIV * DERIV
     tables = jnp.asarray(
         np.stack([split_table(DERIV), split_table(DERIV.T), split_table(square.T)]), BF16
     )
     turner = jnp.asarray(turn_variants(), BF16)
-    shape = jax.ShapeDtypeStruct(source.shape, F32)
+    devices = n_region * n_sub
     vmem = pl.BlockSpec(memory_space=pltpu.VMEM)
     dma = pltpu.SemaphoreType.DMA
-    return pl.pallas_call(
+    smem = pl.BlockSpec(memory_space=pltpu.SMEM)
+    anywhere = pl.BlockSpec(memory_space=pl.ANY)
+    sol, res = pl.pallas_call(
         functools.partial(kernel, n_region, n_sub),
-        out_shape=(shape, shape),
-        in_specs=[vmem] * 10,
+        out_shape=(pltpu.VMEM(source.shape, F32),) * 2,
+        in_specs=[anywhere, anywhere, vmem, smem] + [vmem] * 6,
         out_specs=(vmem, vmem),
         scratch_shapes=[
+            pltpu.VMEM(metric.shape, F32),
             pltpu.VMEM(source.shape, F32),
             pltpu.VMEM(source.shape, F32),
             pltpu.VMEM(source.shape, F32),
@@ -485,18 +475,34 @@
             pltpu.VMEM((ITERS + 1, 4, 64, slots), F32),
             pltpu.VMEM((ITERS + 1, 4, 64, slots), F32),
             pltpu.VMEM((ITERS, 1, 128), F32),
-            pltpu.VMEM((ITERS, n_sub, 1, 128), F32),
-            pltpu.VMEM((ITERS, 1, 128), F32),
-            pltpu.VMEM((ITERS, n_region, 1, 128), F32),
+            pltpu.VMEM((ITERS, devices - 1, 1, 128), F32),
             dma((ITERS + 1, 4)),
             dma((ITERS + 1, 4)),
-            dma((ITERS, n_sub)),
-            dma((ITERS, n_sub)),
-            dma((ITERS, n_region)),
-            dma((ITERS, n_region)),
+            dma((ITERS,)),
+            dma((ITERS,)),
+            dma((4,)),
         ],
         compiler_params=pltpu.CompilerParams(collective_id=0, has_side_effects=True),
-    )(source, metric, face_area, gain, neighbour, orient, outlet, export_list, tables, turner)
+    )(source, metric, face_area, outlet_gain, neighbour, orient, outlet, export_list, tables, turner)
+    shape = jax.ShapeDtypeStruct(source.shape, F32)
+    return pl.pallas_call(
+        write_out,
+        out_shape=(shape, shape),
+        in_specs=[anywhere, anywhere],
+        out_specs=(anywhere, anywhere),
+        scratch_shapes=[dma((2,))],
+    )(pltpu.with_memory_space_constraint(sol, pltpu.VMEM), pltpu.with_memory_space_constraint(res, pltpu.VMEM))
+
+
+def write_out(sol, res, sol_out, res_out, sems):
+    copies = [
+        pltpu.make_async_copy(sol, sol_out, sems.at[0]),
+        pltpu.make_async_copy(res, res_out, sems.at[1]),
+    ]
+    for copy in copies:
+        copy.start()
+    for copy in copies:
+        copy.wait()
 
 
 def solution(mesh):

time: 53.2 us -> 39 us (0.73)
  Pallas kernels: 47.4 us -> 38.1 us
  local copies, waits for them, and re-layouts: 4.91 us -> 0 us
    pallas_call x1 -> x2, Pallas kernels: 47.4 us -> 38.1 us  [the longest x1 37.2 us: per_device(): pl.pallas_call(functools.partial(kernel, n_region, n_sub), out_shape=(plt...]
    unnamed x2 -> x0, local copies, waits for them, and re-layouts: 3.74 us -> none
    pad x1 -> x0, local copies, waits for them, and re-layouts: 1.17 us -> none  [per_device(): jnp.pad(outlet_gain.reshape(1, outlets), ((0, 0), (0, 128 - outlets)))]
where the time goes in v1:
time: 39 us; the launch traced here: 38.8 us
  Pallas kernels  38.1 us (98%)
  between operations  0.64 us (2%)
    pallas_call x1, Pallas kernels, per_device(): pl.pallas_call(functools.partial(kernel, n_region, n_sub), out_shape=(plt...  37.2 us
    pallas_call x1, Pallas kernels, per_device(): pl.pallas_call(write_out, out_shape=(shape, shape), in_specs=[anywhere, a...  0.99 us

profile of v1, /device:TPU:0, one launch (start us, length us, event | category | flops | bytes accessed | tf_op | source)
XLA Modules:
  0.0 38.8 jit_solution(17193076386674577917)
XLA Ops:
  0.6 37.2 %shard_map.113 = (f32[8,8,8,256]{3,2,1,0:T(8,128)S(1)}, f32[8,8,8,256]{3,2,1,0:T(8,128)S(1)}) custom-call(f32[8,8,8,256]{3,2,1,0:T(8,128)} %source_hbm.1, f32[3,8,8,8,256]{4,3,2,1,0:T(8,128)} %metric_hbm.1, f32[6,256]{1,0:T(8,128)} %face_area.1, f32[8]{0:T(128)} %gain.1, s32[6,256]{1,0:T(8,128)} %neighbour.1, s32[6,256]{1,0:T(8,128)} %orient.1, ...), custom_call_target="tpu_custom_call" | custom-call | tf_op jit(solution)/shard_map/pallas_call | solution.py:461
  37.8 1.0 %shard_map.114 = (f32[8,8,8,256]{3,2,1,0:T(8,128)}, f32[8,8,8,256]{3,2,1,0:T(8,128)}) custom-call(f32[8,8,8,256]{3,2,1,0:T(8,128)S(1)} %get-tuple-element.4.sol, f32[8,8,8,256]{3,2,1,0:T(8,128)S(1)} %get-tuple-element.5.res), custom_call_target="tpu_custom_call" | custom-call | tf_op jit(solution)/shard_map/pallas_call | solution.py:488

commit v2 on v1

--- a/solution.py
+++ b/solution.py
@@ -138,7 +138,6 @@
     sub = lax.axis_index("sub")
     square = DERIV * DERIV
     devices = n_region * n_sub
-    me = region * n_sub + sub
 
     loads = [
         pltpu.make_async_copy(metric_hbm.at[0], metric.at[0], load_sem.at[0]),
@@ -153,13 +152,25 @@
 
     barrier = pltpu.get_barrier_semaphore()
 
-    def peer_at(k):
-        peer = lax.rem(me + k, devices)
-        return {"region": lax.div(peer, n_sub), "sub": lax.rem(peer, n_sub)}
-
-    @pl.loop(1, devices)
-    def _(k):
-        pl.semaphore_signal(barrier, inc=1, device_id=peer_at(k), device_id_type=MESH)
+    def wrapped(at, size):
+        return jnp.where(at >= size, at - size, at)
+
+    def every_peer(act):
+        subs = [wrapped(sub + k, n_sub) for k in range(n_sub)]
+        for k in range(1, n_sub):
+            act(k - 1, {"region": region, "sub": subs[k]})
+
+        @pl.loop(1, n_region)
+        def _(step):
+            there = wrapped(region + step, n_region)
+            for k in range(n_sub):
+                act(step * n_sub + k - 1, {"region": there, "sub": subs[k]})
+
+    every_peer(
+        lambda place, peer: pl.semaphore_signal(
+            barrier, inc=1, device_id=peer, device_id_type=MESH
+        )
+    )
 
     chunk = 64
 
@@ -355,16 +366,16 @@
         row = jnp.sum(jnp.where(diag, column, 0.0), axis=0, keepdims=True)
         flux_part[it] = row
 
-        @pl.loop(1, devices)
-        def _(k):
-            pltpu.make_async_remote_copy(
+        every_peer(
+            lambda place, peer: pltpu.make_async_remote_copy(
                 src_ref=flux_part.at[it],
-                dst_ref=flux_recv.at[it, k - 1],
+                dst_ref=flux_recv.at[it, place],
                 send_sem=flux_send_sem.at[it],
                 recv_sem=flux_recv_sem.at[it],
-                device_id=peer_at(k),
+                device_id=peer,
                 device_id_type=MESH,
             ).start()
+        )
 
     def flux_end(it):
         every = flux_recv.at[it]

time: 39 us -> 38.4 us (0.985)
  Pallas kernels: 38.1 us -> 37.6 us
    pallas_call x1, Pallas kernels: 37.2 us -> 36.6 us  [per_device(): pl.pallas_call(functools.partial(kernel, n_region, n_sub), out_shape=(plt...]
where the time goes in v2:
time: 38.4 us; the launch traced here: 38.2 us
  Pallas kernels  37.6 us (98%)
  between operations  0.64 us (2%)
    pallas_call x1, Pallas kernels, per_device(): pl.pallas_call(functools.partial(kernel, n_region, n_sub), out_shape=(plt...  36.6 us
    pallas_call x1, Pallas kernels, per_device(): pl.pallas_call(write_out, out_shape=(shape, shape), in_specs=[anywhere, a...  0.99 us

profile of v2, /device:TPU:0, one launch (start us, length us, event | category | flops | bytes accessed | tf_op | source)
XLA Modules:
  0.0 38.2 jit_solution(325914593235972444)
XLA Ops:
  0.6 36.6 %shard_map.113 = (f32[8,8,8,256]{3,2,1,0:T(8,128)S(1)}, f32[8,8,8,256]{3,2,1,0:T(8,128)S(1)}) custom-call(f32[8,8,8,256]{3,2,1,0:T(8,128)} %source_hbm.1, f32[3,8,8,8,256]{4,3,2,1,0:T(8,128)} %metric_hbm.1, f32[6,256]{1,0:T(8,128)} %face_area.1, f32[8]{0:T(128)} %gain.1, s32[6,256]{1,0:T(8,128)} %neighbour.1, s32[6,256]{1,0:T(8,128)} %orient.1, ...), custom_call_target="tpu_custom_call" | custom-call | tf_op jit(solution)/shard_map/pallas_call | solution.py:472
  37.3 1.0 %shard_map.114 = (f32[8,8,8,256]{3,2,1,0:T(8,128)}, f32[8,8,8,256]{3,2,1,0:T(8,128)}) custom-call(f32[8,8,8,256]{3,2,1,0:T(8,128)S(1)} %get-tuple-element.4.sol, f32[8,8,8,256]{3,2,1,0:T(8,128)S(1)} %get-tuple-element.5.res), custom_call_target="tpu_custom_call" | custom-call | tf_op jit(solution)/shard_map/pallas_call | solution.py:499
